TPU v7x, 128 devices: a whole 4x4x4 slice. The times are simulated.
128 devices in a mesh: gx: 8 (over y_lo, x), gy: 16 (over y_hi, z, core).
Axes of the slice: x: 4, y: 4 (y_hi: 2, y_lo: 2; y = y_hi * 2 + y_lo), z: 4, core: 2. Of those that a mesh axis runs over, the one named last changes fastest.
Arguments:
- patches: bfloat16 [1024, 6144], P('gy', 'gx'), may hold values from -2000 to 2000
- norm_gain: float32 [6144], P('gx'), may hold values from 0.5 to 1.5
- w_up: bfloat16 [6144, 24576], P('gx', 'gy'), may hold values from -0.078125 to 0.078125
- bias_up: float32 [24576], P('gy'), may hold values from -4 to 4
- w_down: bfloat16 [24576, 6144], P('gy', 'gx'), may hold values from -0.0390625 to 0.0390625
- bias_down: float32 [6144], P('gx'), may hold values from -4 to 4
- cotangent: bfloat16 [1024, 6144], P('gy', 'gx'), may hold values from -4 to 4
Outputs:
- mlp_out: bfloat16 [1024, 6144], P('gy', 'gx')
- grad_patches: bfloat16 [1024, 6144], P('gy', 'gx')
- grad_gain: float32 [6144], P('gx')
- grad_w_up: float32 [6144, 24576], P('gx', 'gy')
- grad_bias_up: float32 [24576], P('gy')
- grad_w_down: float32 [24576, 6144], P('gy', 'gx')
- grad_bias_down: float32 [6144], P('gx')
All inputs are finite; a program needn't handle non-finite values.
Results may differ from a plain program's by a relative error of at most 0.007.
Values may be sent and summed in bfloat16 or wider, within the bound.
A program may use at most 128 MiB of HBM per device.

v0:
```python
import jax
import jax.numpy as jnp
from jax import lax
from jax.sharding import PartitionSpec as P

D = 6144


epsilon = 1e-06
inv_root_two = 0.7071067811865476
inv_root_two_pi = 0.3989422804014327


def gelu_value(hidden):
    return 0.5 * hidden * (1.0 + lax.erf(hidden * inv_root_two))


def gelu_slope(hidden):
    return (
        0.5 * (1.0 + lax.erf(hidden * inv_root_two))
        + hidden * jnp.exp(-0.5 * hidden * hidden) * inv_root_two_pi
    )


def over_rows(left, right):
    return lax.dot_general(
        left, right, (((0,), (0,)), ((), ())), preferred_element_type=jnp.float32
    )


def over_cols(left, right):
    return lax.dot_general(
        left, right, (((1,), (1,)), ((), ())), preferred_element_type=jnp.float32
    )


def shards(patches, norm_gain, w_up, bias_up, w_down, bias_down, cotangent):
    values = patches.astype(jnp.float32)
    row_total, row_squares = lax.psum(
        (jnp.sum(values, axis=1), jnp.sum(values * values, axis=1)), "gx"
    )
    row_mean = (row_total / D)[:, None]
    variance = (row_squares / D)[:, None] - row_mean * row_mean
    inv_std = lax.rsqrt(variance + epsilon)
    standard = (values - row_mean) * inv_std
    normed = (standard * norm_gain).astype(jnp.bfloat16)
    partial_value = jnp.dot(
        lax.all_gather(normed, "gy", axis=0, tiled=True), w_up, preferred_element_type=jnp.float32
    )
    hidden = lax.psum(partial_value, "gx") + bias_up
    act_whole = gelu_value(hidden).astype(jnp.bfloat16)
    block = act_whole
    mlp_out = (
        lax.psum_scatter(
            jnp.dot(block, w_down, preferred_element_type=jnp.float32),
            "gy",
            scatter_dimension=0,
            tiled=True,
        )
        + bias_down
    ).astype(jnp.bfloat16)
    piece = lax.all_gather(cotangent, "gy", axis=0, tiled=True)
    weight_total = over_rows(act_whole, piece)
    act_grads = over_cols(piece, w_down)
    grad_act = lax.psum(act_grads, "gx")
    grad_whole = (grad_act * gelu_slope(hidden)).astype(jnp.bfloat16)
    grad_bias_up = jnp.sum(grad_whole, axis=0, dtype=jnp.float32)
    grad_w_up = over_rows(lax.all_gather(normed, "gy", axis=0, tiled=True), grad_whole)
    block = grad_whole
    grad_normed = lax.psum_scatter(over_cols(block, w_up), "gy", scatter_dimension=0, tiled=True)
    grad_gain, grad_bias_down = lax.psum(
        (jnp.sum(grad_normed * standard, axis=0), jnp.sum(cotangent, axis=0, dtype=jnp.float32)),
        "gy",
    )
    scaled = grad_normed * norm_gain
    first_total, second_total = lax.psum(
        (jnp.sum(scaled, axis=1), jnp.sum(scaled * standard, axis=1)), "gx"
    )
    first_mean = (first_total / D)[:, None]
    second_mean = (second_total / D)[:, None]
    grad_patches = (inv_std * (scaled - first_mean - standard * second_mean)).astype(jnp.bfloat16)
    return (mlp_out, grad_patches, grad_gain, grad_w_up, grad_bias_up, weight_total, grad_bias_down)


def solution(mesh):
    in_specs = (
        P("gy", "gx"),
        P("gx"),
        P("gx", "gy"),
        P("gy"),
        P("gy", "gx"),
        P("gx"),
        P("gy", "gx"),
    )
    out_specs = (
        P("gy", "gx"),
        P("gy", "gx"),
        P("gx"),
        P("gx", "gy"),
        P("gy"),
        P("gy", "gx"),
        P("gx"),
    )
    return jax.shard_map(shards, mesh=mesh, in_specs=in_specs, out_specs=out_specs, check_vma=False)
```

profile of v0, /device:TPU:1, one launch (start us, length us, event | category | flops | bytes accessed | tf_op | source)
XLA Modules:
  0.0 569.6 jit_solution(7899502057630705862)
XLA Ops:
  7.2 0.0 all-gather.3.cloned.1.call-start
  7.2 1.2 convert_reduce_fusion.1
  8.4 16.8 %all-reduce.2 = (f32[64]{0:T(128)S(1)}, f32[64]{0:T(128)S(1)}) all-reduce(f32[64]{0:T(128)S(1)} %get-tuple-element.11, f32[64]{0:T(128)S(1)} %get-tuple-element.10), channel_id=1, replica_groups=mesh['gx'=8,'gy'=16] {'gx'}, use_global_device_ids=true, to_apply=%region_3.0 | all-reduce | flops 128 | bytes 1024 | tf_op jit(solution)/shard_map/psum | solution.py:39
  25.2 1.6 fusion.11
  26.8 0.0 all-gather.3.cloned.1.call-update
  26.9 0.0 all-gather.5.cloned.1.call-start
  26.9 0.7 all-gather.5.cloned.1.call-update
  27.6 0.0 all-reduce.6.cloned.1.call-start
  27.7 49.5 %all-gather.3.cloned.1.call-done = bf16[1024,768]{1,0:T(8,128)(2,1)} async-done(((bf16[64,768]{1,0:T(8,128)(2,1)}), bf16[1024,768]{1,0:T(8,128)(2,1)}) %all-gather.3.cloned.1.call-update) | async-done | bytes 1572880 | tf_op jit(solution)/shard_map/all_gather | solution.py:48
  77.2 5.9 %fusion.19 = f32[1024,1536]{1,0:T(8,128)} fusion(bf16[1024,768]{1,0:T(8,128)(2,1)} %all-gather.3.cloned.1.call-done, bf16[768,1536]{1,0:T(8,128)(2,1)S(1)} %copy-done), kind=kOutput, calls=%fused_computation.32 | convolution fusion | flops 2415919104 | bytes 10223616 | tf_op jit(solution)/shard_map/dot_general | solution.py:47
  83.1 41.7 %all-gather.5.cloned.1.call-done = bf16[1024,768]{1,0:T(8,128)(2,1)} async-done(((bf16[64,768]{1,0:T(8,128)(2,1)}), bf16[1024,768]{1,0:T(8,128)(2,1)}) %all-gather.5.cloned.1.call-update) | async-done | bytes 1572880 | tf_op jit(solution)/shard_map/all_gather | solution.py:62
  124.8 7.4 %fusion.21 = f32[1024,1536]{1,0:T(8,128)} fusion(bf16[1024,768]{1,0:T(8,128)(2,1)} %all-gather.5.cloned.1.call-done, bf16[1536,768]{1,0:T(8,128)(2,1)} %param.11), kind=kOutput, calls=%fused_computation.34 | convolution fusion | flops 2415919104 | bytes 10223616 | tf_op jit(solution)/shard_map/dot_general | solution.py:32
  132.2 0.0 all-reduce.6.cloned.1.call-update
  132.2 0.0 reduce-scatter.5.cloned.1.call-start
  132.3 262.0 %all-reduce.6.cloned.1.call-done = (f32[1024,1536]{1,0:T(8,128)}, f32[1024,1536]{1,0:T(8,128)}) async-done(((f32[1024,1536]{1,0:T(8,128)}, f32[1024,1536]{1,0:T(8,128)}), (f32[1024,1536]{1,0:T(8,128)}, f32[1024,1536]{1,0:T(8,128)})) %all-reduce.6.cloned.1.call-update) | async-done | bytes 12582928 | tf_op jit(solution)/shard_map/psum | solution.py:50
  394.3 9.2 %convert_reduce_fusion = (f32[1536]{0:T(1024)}, bf16[1024,1536]{1,0:T(8,128)(2,1)S(1)}, bf16[1024,1536]{1,0:T(8,128)(2,1)}) fusion(f32[1024,1536]{1,0:T(8,128)} %get-tuple-element.19, f32[1024,1536]{1,0:T(8,128)} %get-tuple-element.18, f32[1536]{0:T(1024)S(1)} %copy-done.6), kind=kLoop, calls=%fused_computation.7 | loop fusion | flops 25164288 | bytes 18886656 | tf_op jit(solution)/shard_map/reduce_sum | solution.py:67
  403.5 1.7 copy-done.1
  405.2 4.3 fusion.22
  409.5 0.0 reduce-scatter.5.cloned.1.call-update
  409.5 0.0 reduce-scatter.3.cloned.1.call-start
  409.6 6.9 %fusion.20 = f32[1024,768]{1,0:T(8,128)} fusion(bf16[1024,1536]{1,0:T(8,128)(2,1)} %get-tuple-element.22, bf16[1536,768]{1,0:T(8,128)(2,1)} %param.11), kind=kOutput, calls=%fused_computation.33 | convolution fusion | flops 2415919104 | bytes 8650752 | tf_op jit(solution)/shard_map/dot_general | solution.py:55
  416.5 0.0 reduce-scatter.3.cloned.1.call-update
  416.5 0.9 copy-done.4
  417.4 7.5 %fusion.23 = f32[768,1536]{1,0:T(8,128)} fusion(bf16[1024,768]{1,0:T(8,128)(2,1)} %all-gather.3.cloned.1.call-done, bf16[1024,1536]{1,0:T(8,128)(2,1)} %copy-done.1), kind=kOutput, calls=%fused_computation.36 | convolution fusion | flops 2415919104 | bytes 9437184 | tf_op jit(solution)/shard_map/dot_general | solution.py:26
  425.0 4.4 fusion.24
  429.4 53.7 %reduce-scatter.5.cloned.1.call-done = f32[64,768]{1,0:T(8,128)} async-done(((f32[1024,768]{1,0:T(8,128)}), f32[64,768]{1,0:T(8,128)}) %reduce-scatter.5.cloned.1.call-update) | async-done | bytes 196624 | tf_op jit(solution)/shard_map/reduce_scatter | solution.py:70
  483.1 1.2 fusion.16
  484.3 14.9 %all-reduce.1 = (f32[64]{0:T(128)S(1)}, f32[64]{0:T(128)S(1)}) all-reduce(f32[64]{0:T(128)S(1)} %get-tuple-element.8, f32[64]{0:T(128)S(1)} %get-tuple-element.9), channel_id=1, replica_groups=mesh['gx'=8,'gy'=16] {'gx'}, use_global_device_ids=true, to_apply=%region_11.0 | all-reduce | flops 128 | bytes 1024 | tf_op jit(solution)/shard_map/psum | solution.py:76
  499.2 39.6 %all-reduce = (f32[768]{0:T(1024)}, f32[768]{0:T(1024)}) all-reduce(f32[768]{0:T(1024)S(1)} %get-tuple-element.7, f32[768]{0:T(1024)S(1)} %convert_reduce_fusion.2), channel_id=1, replica_groups=mesh['gx'=8,'gy'=16] {'gy'}, use_global_device_ids=true, to_apply=%region_13.0 | all-reduce | flops 1536 | bytes 12288 | tf_op jit(solution)/shard_map/psum | solution.py:71
  538.8 1.7 fusion.15
  540.5 21.1 %reduce-scatter.3.cloned.1.call-done = f32[64,768]{1,0:T(8,128)} async-done(((f32[1024,768]{1,0:T(8,128)}), f32[64,768]{1,0:T(8,128)}) %reduce-scatter.3.cloned.1.call-update) | async-done | bytes 196624 | tf_op jit(solution)/shard_map/reduce_scatter | solution.py:54
  561.5 1.6 add_convert_fusion
  (19 shorter events, 0.1 us)
Async XLA Ops:
  7.2 70.0 %copy-start = (bf16[768,1536]{1,0:T(8,128)(2,1)S(1)}, bf16[768,1536]{1,0:T(8,128)(2,1)}, u32[]{:S(2)}) copy-start(bf16[768,1536]{1,0:T(8,128)(2,1)} %param.9) | copy-start | bytes 7077892
  7.2 70.0 %all-gather.3.cloned.1.call-start = ((), (), s32[]{:S(2)}) async-start(), calls=%async_computation.2 | async-start | bytes 1671168 | tf_op jit(solution)/shard_map/all_gather | solution.py:48
  26.9 98.0 %all-gather.5.cloned.1.call-start = ((), (), s32[]{:S(2)}) async-start(), calls=%async_computation.4 | async-start | bytes 1671168 | tf_op jit(solution)/shard_map/all_gather | solution.py:62
  27.6 366.7 %all-reduce.6.cloned.1.call-start = ((), (), s32[]{:S(2)}) async-start(), calls=%async_computation.6 | async-start | bytes 25165824 | tf_op jit(solution)/shard_map/psum | solution.py:50
  132.2 262.1 %copy-start.6 = (f32[1536]{0:T(1024)S(1)}, f32[1536]{0:T(1024)}, u32[]{:S(2)}) copy-start(f32[1536]{0:T(1024)} %param.10) | copy-start | bytes 18436
  132.2 350.9 %reduce-scatter.5.cloned.1.call-start = ((), (), s32[]{:S(2)}) async-start(), calls=%async_computation.5 | async-start | bytes 3342336 | tf_op jit(solution)/shard_map/reduce_scatter | solution.py:70
  403.5 1.7 copy-start.1
  409.5 152.0 %reduce-scatter.3.cloned.1.call-start = ((), (), s32[]{:S(2)}) async-start(), calls=%async_computation.3 | async-start | bytes 3342336 | tf_op jit(solution)/shard_map/reduce_scatter | solution.py:54
  416.5 0.9 copy-start.4
  417.4 7.5 %copy-start.2 = (bf16[1024,1536]{1,0:T(8,128)(2,1)S(1)}, bf16[1024,1536]{1,0:T(8,128)(2,1)}, u32[]{:S(2)}) copy-start(bf16[1024,1536]{1,0:T(8,128)(2,1)} %get-tuple-element.22) | copy-start | bytes 9437188
  417.4 7.5 %copy-start.8 = (bf16[1024,768]{1,0:T(8,128)(2,1)S(1)}, bf16[1024,768]{1,0:T(8,128)(2,1)}, u32[]{:S(2)}) copy-start(bf16[1024,768]{1,0:T(8,128)(2,1)} %all-gather.5.cloned.1.call-done) | copy-start | bytes 4718596
  424.9 58.1 %copy-start.3 = (bf16[64,768]{1,0:T(8,128)(2,1)S(1)}, bf16[64,768]{1,0:T(8,128)(2,1)}, u32[]{:S(2)}) copy-start(bf16[64,768]{1,0:T(8,128)(2,1)} %param.7) | copy-start | bytes 294916
  425.0 58.1 %copy-start.5 = (f32[768]{0:T(1024)S(1)}, f32[768]{0:T(1024)}, u32[]{:S(2)}) copy-start(f32[768]{0:T(1024)} %param.8) | copy-start | bytes 9220
  425.0 136.6 %copy-start.7 = (f32[768]{0:T(1024)S(1)}, f32[768]{0:T(1024)}, u32[]{:S(2)}) copy-start(f32[768]{0:T(1024)} %param.12) | copy-start | bytes 9220
Sparse Core Ops, SparseCore 0:
  27.0 50.1 all-gather.2
  79.7 45.0 all-gather.4
  132.3 261.9 all-reduce.5
  409.7 73.3 reduce-scatter.4
  487.0 74.4 reduce-scatter.2
where the time goes:
time: 570 us
  waiting for transfers between devices  429 us (75%)
  blocking collectives  71.3 us (13%)
  matrix products  36.4 us (6%)
  other arithmetic  16.4 us (3%)
  between operations  13.8 us (2%)
    psum x1, waiting for transfers between devices, shards(): hidden = lax.psum(partial_value, 'gx') + bias_up  262 us
    reduce_scatter x1, waiting for transfers between devices, shards(): lax.psum_scatter(over_cols(block, w_up), 'gy', scatter_dimension=0, tiled...  53.7 us
    all_gather x1, waiting for transfers between devices, shards(): lax.all_gather(normed, 'gy', axis=0, tiled=True)  49.5 us
    all_gather x1, waiting for transfers between devices, shards(): piece = lax.all_gather(cotangent, 'gy', axis=0, tiled=True)  41.7 us
    psum x1, blocking collectives, shards(): lax.psum((jnp.sum(grad_normed * standard, axis=0), jnp.sum(cotangent, axi...  39.6 us
    reduce_scatter x1, waiting for transfers between devices, shards(): lax.psum_scatter(jnp.dot(block, w_down, preferred_element_type=jnp.float3...  21.1 us
    psum x1, blocking collectives, shards(): lax.psum((jnp.sum(values, axis=1), jnp.sum(values * values, axis=1)), 'gx')  16.8 us
    psum x1, blocking collectives, shards(): lax.psum((jnp.sum(scaled, axis=1), jnp.sum(scaled * standard, axis=1)), '...  14.9 us
  transfers between devices with their start and end apart: 5, of which 5 were waited for; matrix products, arithmetic and copies ran while one was open for 5% of the time, Pallas kernels for 0%

commit v1 on v0

v1 whole, which is shorter than its diff:
```python
import functools

import jax
import jax.numpy as jnp
from jax import lax
from jax.experimental import pallas as pl
from jax.experimental.pallas import tpu as pltpu
from jax.sharding import PartitionSpec as P

D = 6144
CHUNKS = 4
MESSAGES = 240

epsilon = 1e-06
inv_root_two = 0.7071067811865476
inv_root_two_pi = 0.3989422804014327

MESH = pl.DeviceIdType.MESH
F32 = jnp.float32
BF16 = jnp.bfloat16


def wide(value):
    return value.astype(F32)


class Mail:
    def __init__(self, send_sems, recv_sems):
        self.send_sems, self.recv_sems, self.sent = send_sems, recv_sems, []

    def send(self, src, dst, device):
        at = len(self.sent)
        copy = pltpu.make_async_remote_copy(
            src_ref=src,
            dst_ref=dst,
            send_sem=self.send_sems.at[at],
            recv_sem=self.recv_sems.at[at],
            device_id=device,
            device_id_type=MESH,
        )
        copy.start()
        self.sent.append(copy)
        return copy

    def finish(self):
        for copy in self.sent:
            copy.wait_send()


def kernel(
    patches, gain, w_up, bias_up, w_down, bias_down, cotangent,
    mlp_out, grad_patches, grad_gain, grad_w_up, grad_bias_up, grad_w_down, grad_bias_down,
    own, standard, wu, wd, cot_all, nor_all,
    ga, ga_y, ga_m1r, ga_m1l, ga_l, ga_r,
    hid, hid_m1r, hid_m1l, hid_l, hid_r, hid_ys, hid_y,
    act, gh,
    mlp_g, mlp_sib, mlp_z, mlp_ys, mlp_y,
    gn_g, gn_sib, gn_z, gn_ys, gn_y, gn,
    stats_a, stats_b, gains, gwu, gwd,
    local_sems, send_sems, recv_sems,
):
    gx, gy = lax.axis_index("gx"), lax.axis_index("gy")
    x, y = lax.rem(gx, 4), lax.div(gx, 4)
    k, z, yh = lax.rem(gy, 2), lax.rem(lax.div(gy, 2), 4), lax.div(gy, 8)
    yo, ko, yho = 1 - y, 1 - k, 1 - yh
    xr, xo, xl = lax.rem(x + 1, 4), lax.rem(x + 2, 4), lax.rem(x + 3, 4)
    right, left, across = (y * 4 + xr, gy), (y * 4 + xl, gy), (yo * 4 + x, gy)
    sibling, far = (gx, yh * 8 + z * 2 + ko), (gx, yho * 8 + z * 2 + k)
    z_at = [lax.rem(z + d, 4) for d in range(4)]
    z_dev = [(gx, yh * 8 + z_at[d] * 2 + k) for d in range(4)]
    mail = Mail(send_sems, recv_sems)

    loads = [pltpu.make_async_copy(patches, own, local_sems.at[0])]
    for c in range(CHUNKS):
        loads.append(
            pltpu.make_async_copy(
                cotangent.at[pl.ds(16 * c, 16)], cot_all.at[c, yh, z, k], local_sems.at[1 + c]
            )
        )
    load_wd = pltpu.make_async_copy(w_down, wd, local_sems.at[5])
    load_wu = pltpu.make_async_copy(w_up, wu, local_sems.at[6])
    for copy in loads + [load_wd, load_wu]:
        copy.start()

    barrier = pltpu.get_barrier_semaphore()
    for d in range(1, 8):
        pl.semaphore_signal(barrier, inc=1, device_id=(lax.rem(gx + d, 8), gy), device_id_type=MESH)
    for d in range(1, 16):
        pl.semaphore_signal(barrier, inc=1, device_id=(gx, lax.rem(gy + d, 16)), device_id_type=MESH)
    pl.semaphore_wait(barrier, 22)

    far_in, z_in, sib_in = {}, {}, {}

    def to_far(name, full, c):
        piece = full.at[c, yh, z, k]
        far_in[name, c] = mail.send(piece, piece, far)

    def to_z(name, full, c):
        far_in[name, c].wait_recv()
        pair = full.at[c, :, z, k]
        z_in[name, c] = [mail.send(pair, pair, z_dev[d]) for d in (1, 2, 3)]

    def to_sibling(name, full, c):
        for copy in z_in[name, c]:
            copy.wait_recv()
        half = full.at[c, :, :, k]
        sib_in[name, c] = mail.send(half, half, sibling)

    def post_stats(box, first, second):
        lane = lax.broadcasted_iota(jnp.int32, (64, 128), 1)
        table = jnp.where(lane == 0, first, jnp.where(lane == 1, second, 0.0))
        table = jnp.concatenate([table, jnp.zeros((64, 128), F32)], axis=0)
        box[gx] = jnp.transpose(table)[:8]
        mine = box.at[gx]
        return [mail.send(mine, mine, (lax.rem(gx + d, 8), gy)) for d in range(1, 8)]

    def read_stats(box, copies):
        for copy in copies:
            copy.wait_recv()
        total = jnp.sum(box[...], axis=0)
        table = jnp.transpose(jnp.concatenate([total, jnp.zeros((120, 128), F32)], axis=0))
        return table[:64, 0:1] / D, table[:64, 1:2] / D

    for c in range(CHUNKS):
        loads[1 + c].wait()
        to_far("cot", cot_all, c)
    loads[0].wait()
    values = wide(own[...])
    stats = post_stats(
        stats_a,
        jnp.sum(values, axis=1, keepdims=True),
        jnp.sum(values * values, axis=1, keepdims=True),
    )

    def columns(total, step, body):
        @pl.loop(0, total // step)
        def _(n):
            body(pl.ds(pl.multiple_of(n * step, step), step))

    def multiply(left_value, right_ref, transposed, out, c, shape, total, step):
        def body(cols):
            if transposed:
                product = lax.dot_general(
                    left_value(), right_ref[cols, :], (((1,), (1,)), ((), ())),
                    preferred_element_type=F32,
                )
            else:
                product = jnp.dot(left_value(), right_ref[:, cols], preferred_element_type=F32)
            out[(c,) + (slice(None),) * (len(shape)) + (cols,)] = product.astype(BF16).reshape(
                shape + (step,)
            )

        columns(total, step, body)

    rows_gx, rows_gy = (4, 2, 32), (2, 4, 2, 16)

    def make_ga(c):
        sib_in["cot", c].wait_recv()
        if c == 0:
            load_wd.wait()
        multiply(lambda: cot_all[c].reshape(256, 768), wd, True, ga, c, rows_gx, 1536, 512)

    def make_hid(c):
        sib_in["nor", c].wait_recv()
        if c == 0:
            load_wu.wait()
        multiply(lambda: nor_all[c].reshape(256, 768), wu, False, hid, c, rows_gx, 1536, 512)

    def make_mlp(c):
        multiply(lambda: act[c].reshape(256, 1536), wd, False, mlp_g, c, rows_gy, 768, 256)

    def make_gn(c):
        multiply(lambda: gh[c].reshape(256, 1536), wu, True, gn_g, c, rows_gy, 768, 256)

    def weight_grad(out, left_ref, right_ref, c, rows, width):
        right_width = 768 + 1536 - rows

        def body(n):
            cols = pl.ds(pl.multiple_of(n * width, width), width)
            left_value = left_ref[(c,) + (slice(None),) * (len(left_ref.shape) - 2) + (cols,)]
            product = lax.dot_general(
                left_value.reshape(256, width), right_ref[c].reshape(256, right_width),
                (((0,), (0,)), ((), ())), preferred_element_type=F32,
            )
            if c == 0:
                out[cols, :] = product
            else:
                out[cols, :] += product

        pl.loop(0, rows // width)(body)

    ga_in, hid_in, act_in, gh_in = {}, {}, {}, {}
    top, low = pl.ds(0, 16), pl.ds(16, 16)

    def ga1(c):
        ga_in[c] = [mail.send(ga.at[c, :, yo], ga_y.at[c], across)]

    def ga2(c):
        ga_in[c][0].wait_recv()
        for t in (xo, xr, xl):
            ga[c, t, y] = (wide(ga[c, t, y]) + wide(ga_y[c, t])).astype(BF16)
        ga_in[c] = [
            mail.send(ga.at[c, xo, y, top], ga_m1r.at[c], right),
            mail.send(ga.at[c, xo, y, low], ga_m1l.at[c], left),
            mail.send(ga.at[c, xr, y, low], ga_l.at[c, low], right),
            mail.send(ga.at[c, xl, y, top], ga_r.at[c, top], left),
        ]

    def ga3(c):
        ga_in[c][0].wait_recv()
        ga[c, xr, y, top] = (wide(ga[c, xr, y, top]) + wide(ga_m1r[c])).astype(BF16)
        first = mail.send(ga.at[c, xr, y, top], ga_l.at[c, top], right)
        ga_in[c][1].wait_recv()
        ga[c, xl, y, low] = (wide(ga[c, xl, y, low]) + wide(ga_m1l[c])).astype(BF16)
        second = mail.send(ga.at[c, xl, y, low], ga_r.at[c, low], left)
        ga_in[c] = ga_in[c][2:] + [first, second]

    def ga4(c):
        for copy in ga_in[c]:
            copy.wait_recv()

    def hid1(c):
        hid_in[c] = [
            mail.send(hid.at[c, xo, 0], hid_m1r.at[c], right),
            mail.send(hid.at[c, xo, 1], hid_m1l.at[c], left),
            mail.send(hid.at[c, xr, 1], hid_l.at[c, 1], right),
            mail.send(hid.at[c, xl, 0], hid_r.at[c, 0], left),
        ]

    def hid2(c):
        hid_in[c][0].wait_recv()
        hid[c, xr, 0] = (wide(hid[c, xr, 0]) + wide(hid_m1r[c])).astype(BF16)
        first = mail.send(hid.at[c, xr, 0], hid_l.at[c, 0], right)
        hid_in[c][1].wait_recv()
        hid[c, xl, 1] = (wide(hid[c, xl, 1]) + wide(hid_m1l[c])).astype(BF16)
        second = mail.send(hid.at[c, xl, 1], hid_r.at[c, 1], left)
        hid_in[c] = hid_in[c][2:] + [first, second]

    def hid_sum(c, at):
        return wide(hid[c, x, at]) + wide(hid_l[c, at]) + wide(hid_r[c, at])

    def hid3(c):
        for copy in hid_in[c]:
            copy.wait_recv()
        hid_ys[c] = hid_sum(c, yo).astype(BF16)
        hid_in[c] = [mail.send(hid_ys.at[c], hid_y.at[c], across)]

    def hid4(c):
        hid_in[c][0].wait_recv()

    def activate(c):
        ga4(c)
        hid4(c)
        hidden = hid_sum(c, y) + wide(hid_y[c]) + bias_up[...]
        phi = 0.5 * (1.0 + lax.erf(hidden * inv_root_two))
        act[c, x, y] = (hidden * phi).astype(BF16)
        total = wide(ga[c, x, y]) + wide(ga_y[c, x]) + wide(ga_l[c]) + wide(ga_r[c])
        slope = phi + hidden * jnp.exp(-0.5 * hidden * hidden) * inv_root_two_pi
        gh[c, x, y] = (total * slope).astype(BF16)

    def act1(c):
        piece = act.at[c, x, y]
        act_in[c] = [mail.send(piece, piece, device) for device in (across, right, left)]

    def act2(c):
        act_in[c][0].wait_recv()
        piece = act.at[c, x, yo]
        act_in[c] = act_in[c][1:] + [mail.send(piece, piece, device) for device in (right, left)]

    def act3(c):
        for copy in act_in[c]:
            copy.wait_recv()
        act_in[c] = [
            mail.send(act.at[c, xl, 0], act.at[c, xl, 0], right),
            mail.send(act.at[c, xr, 1], act.at[c, xr, 1], left),
        ]

    def act4(c):
        for copy in act_in[c]:
            copy.wait_recv()

    def gh1(c):
        piece = gh.at[c, x, y]
        gh_in[c] = [mail.send(piece, piece, device) for device in (right, left, across)]

    def gh2(c):
        from_left, from_right, from_across = gh_in[c]
        from_left.wait_recv()
        first = mail.send(gh.at[c, xl, y, top], gh.at[c, xl, y, top], right)
        across_left = mail.send(gh.at[c, xl, y], gh.at[c, xl, y], across)
        from_right.wait_recv()
        second = mail.send(gh.at[c, xr, y, low], gh.at[c, xr, y, low], left)
        across_right = mail.send(gh.at[c, xr, y], gh.at[c, xr, y], across)
        gh_in[c] = [first, second, from_across, across_left, across_right]

    def gh3(c):
        gh_in[c][0].wait_recv()
        gh_in[c][1].wait_recv()
        gh_in[c] = gh_in[c][2:] + [mail.send(gh.at[c, xo, y], gh.at[c, xo, y], across)]

    def gh4(c):
        for copy in gh_in[c]:
            copy.wait_recv()

    boxes = {"mlp": (mlp_g, mlp_sib, mlp_z, mlp_ys, mlp_y), "gn": (gn_g, gn_sib, gn_z, gn_ys, gn_y)}
    back = {}

    def back0(name, c):
        part, sib, _, _, _ = boxes[name]
        back[name, c] = mail.send(part.at[c, :, :, ko], sib.at[c], sibling)

    def back1(name, c):
        part, sib, z_box, _, _ = boxes[name]
        back[name, c].wait_recv()
        part[c, :, :, k] = (wide(part[c, :, :, k]) + wide(sib[c])).astype(BF16)
        back[name, c] = [
            mail.send(part.at[c, :, z_at[d], k], z_box.at[c, z], z_dev[d]) for d in (1, 2, 3)
        ]

    def back_sum(name, c, at):
        part, _, z_box, _, _ = boxes[name]
        total = wide(part[c, at, z, k])
        for d in (1, 2, 3):
            total = total + wide(z_box[c, z_at[d], at])
        return total

    def back2(name, c):
        _, _, _, ys, y_box = boxes[name]
        for copy in back[name, c]:
            copy.wait_recv()
        ys[c] = back_sum(name, c, yho).astype(BF16)
        back[name, c] = mail.send(ys.at[c], y_box.at[c], far)

    def back3(name, c):
        back[name, c].wait_recv()
        total = back_sum(name, c, yh) + wide(boxes[name][4][c])
        if name == "mlp":
            mlp_out[pl.ds(16 * c, 16), :] = (total + bias_down[...]).astype(BF16)
        else:
            gn[pl.ds(16 * c, 16), :] = total

    for c in range(CHUNKS):
        to_z("cot", cot_all, c)
    row_mean, square_mean = read_stats(stats_a, stats)
    inv_std = lax.rsqrt(square_mean - row_mean * row_mean + epsilon)
    normal = (values - row_mean) * inv_std
    standard[...] = normal
    normed = (normal * gain[...]).astype(BF16)
    for c in range(CHUNKS):
        nor_all[c, yh, z, k] = normed[16 * c : 16 * c + 16]
        to_far("nor", nor_all, c)

    def cot3(c):
        to_sibling("cot", cot_all, c)

    def nor3(c):
        to_sibling("nor", nor_all, c)

    def start_ga(c):
        make_ga(c)
        ga1(c)

    def start_hid(c):
        make_hid(c)
        hid1(c)

    def start_act(c):
        activate(c)
        act1(c)
        gh1(c)

    def start_mlp(c):
        act4(c)
        make_mlp(c)
        back0("mlp", c)

    def start_gn(c):
        gh4(c)
        make_gn(c)
        back0("gn", c)

    def grad_down(c):
        weight_grad(gwd, act, cot_all, c, 1536, 256)

    def grad_up(c):
        weight_grad(gwu, nor_all, gh, c, 768, 256)

    cot3(0)
    start_ga(0)
    cot3(1)
    for c in range(CHUNKS):
        to_z("nor", nor_all, c)
    start_ga(1)
    cot3(2)
    nor3(0)
    ga2(0)
    start_hid(0)
    start_ga(2)
    cot3(3)
    nor3(1)
    ga3(0)
    ga2(1)
    hid2(0)
    start_hid(1)
    start_ga(3)
    nor3(2)
    ga3(1)
    ga2(2)
    hid3(0)
    hid2(1)
    start_hid(2)
    start_act(0)
    nor3(3)
    ga3(2)
    ga2(3)
    hid3(1)
    hid2(2)
    act2(0)
    start_hid(3)
    start_act(1)
    gh2(0)
    ga3(3)
    hid3(2)
    hid2(3)
    act3(0)
    act2(1)
    start_act(2)
    gh3(0)
    gh2(1)
    hid3(3)
    start_mlp(0)
    act3(1)
    act2(2)
    start_act(3)
    start_gn(0)
    grad_down(0)
    gh3(1)
    gh2(2)
    back1("mlp", 0)
    start_mlp(1)
    act3(2)
    act2(3)
    back1("gn", 0)
    grad_up(0)
    start_gn(1)
    gh3(2)
    gh2(3)
    back2("mlp", 0)
    back1("mlp", 1)
    grad_down(1)
    start_mlp(2)
    act3(3)
    back2("gn", 0)
    back1("gn", 1)
    start_gn(2)
    gh3(3)
    grad_up(1)
    back3("mlp", 0)
    back2("mlp", 1)
    back1("mlp", 2)
    start_mlp(3)
    grad_down(2)
    back3("gn", 0)
    back2("gn", 1)
    back1("gn", 2)
    grad_up(2)
    back3("mlp", 1)
    back2("mlp", 2)
    start_gn(3)
    back1("mlp", 3)
    grad_down(3)
    store_wd = pltpu.make_async_copy(gwd, grad_w_down, local_sems.at[7])
    store_wd.start()
    back3("gn", 1)
    back2("gn", 2)
    back1("gn", 3)
    back3("mlp", 2)
    back2("mlp", 3)
    back3("gn", 2)
    grad_up(3)
    store_wu = pltpu.make_async_copy(gwu, grad_w_up, local_sems.at[8])
    store_wu.start()
    back2("gn", 3)
    back3("mlp", 3)
    back3("gn", 3)

    grad_normed = gn[...]
    normal = standard[...]
    weighted = grad_normed * normal
    gains[gy] = jnp.sum(weighted.reshape(8, 8, 768), axis=0)
    scaled = grad_normed * gain[...]
    stats = post_stats(
        stats_b,
        jnp.sum(scaled, axis=1, keepdims=True),
        jnp.sum(scaled * normal, axis=1, keepdims=True),
    )
    mine = gains.at[gy]
    gain_in = [mail.send(mine, mine, (gx, lax.rem(gy + d, 16))) for d in range(1, 16)]
    total = jnp.zeros((1, 768), F32)
    for c in range(CHUNKS):
        total = total + jnp.sum(wide(cot_all[c].reshape(256, 768)), axis=0, keepdims=True)
    grad_bias_down[...] = total
    total = jnp.zeros((1, 1536), F32)
    for c in range(CHUNKS):
        total = total + jnp.sum(wide(gh[c].reshape(256, 1536)), axis=0, keepdims=True)
    grad_bias_up[...] = total
    first_mean, second_mean = read_stats(stats_b, stats)
    scaled = gn[...] * gain[...]
    grad_patches[...] = (inv_std * (scaled - first_mean - standard[...] * second_mean)).astype(BF16)
    for copy in gain_in:
        copy.wait_recv()
    grad_gain[...] = jnp.sum(jnp.sum(gains[...], axis=0), axis=0, keepdims=True)
    mail.finish()
    store_wd.wait()
    store_wu.wait()


def shards(patches, norm_gain, w_up, bias_up, w_down, bias_down, cotangent):
    hbm, vmem = pl.BlockSpec(memory_space=pl.ANY), pl.BlockSpec(memory_space=pltpu.VMEM)
    shape = jax.ShapeDtypeStruct
    scratch = [
        pltpu.VMEM((64, 768), BF16),
        pltpu.VMEM((64, 768), F32),
        pltpu.VMEM((768, 1536), BF16),
        pltpu.VMEM((1536, 768), BF16),
        pltpu.VMEM((4, 2, 4, 2, 16, 768), BF16),
        pltpu.VMEM((4, 2, 4, 2, 16, 768), BF16),
        pltpu.VMEM((4, 4, 2, 32, 1536), BF16),
        pltpu.VMEM((4, 4, 32, 1536), BF16),
        pltpu.VMEM((4, 16, 1536), BF16),
        pltpu.VMEM((4, 16, 1536), BF16),
        pltpu.VMEM((4, 32, 1536), BF16),
        pltpu.VMEM((4, 32, 1536), BF16),
        pltpu.VMEM((4, 4, 2, 32, 1536), BF16),
        pltpu.VMEM((4, 32, 1536), BF16),
        pltpu.VMEM((4, 32, 1536), BF16),
        pltpu.VMEM((4, 2, 32, 1536), BF16),
        pltpu.VMEM((4, 2, 32, 1536), BF16),
        pltpu.VMEM((4, 32, 1536), BF16),
        pltpu.VMEM((4, 32, 1536), BF16),
        pltpu.VMEM((4, 4, 2, 32, 1536), BF16),
        pltpu.VMEM((4, 4, 2, 32, 1536), BF16),
    ]
    for _ in range(2):
        scratch += [
            pltpu.VMEM((4, 2, 4, 2, 16, 768), BF16),
            pltpu.VMEM((4, 2, 4, 16, 768), BF16),
            pltpu.VMEM((4, 4, 2, 16, 768), BF16),
            pltpu.VMEM((4, 16, 768), BF16),
            pltpu.VMEM((4, 16, 768), BF16),
        ]
    scratch += [
        pltpu.VMEM((64, 768), F32),
        pltpu.VMEM((8, 8, 128), F32),
        pltpu.VMEM((8, 8, 128), F32),
        pltpu.VMEM((16, 8, 768), F32),
        pltpu.VMEM((768, 1536), F32),
        pltpu.VMEM((1536, 768), F32),
        pltpu.SemaphoreType.DMA((9,)),
        pltpu.SemaphoreType.DMA((MESSAGES,)),
        pltpu.SemaphoreType.DMA((MESSAGES,)),
    ]
    outs = pl.pallas_call(
        kernel,
        out_shape=(
            shape((64, 768), BF16),
            shape((64, 768), BF16),
            shape((1, 768), F32),
            shape((768, 1536), F32),
            shape((1, 1536), F32),
            shape((1536, 768), F32),
            shape((1, 768), F32),
        ),
        in_specs=[hbm, vmem, hbm, vmem, hbm, vmem, hbm],
        out_specs=(vmem, vmem, vmem, hbm, vmem, hbm, vmem),
        scratch_shapes=scratch,
        compiler_params=pltpu.CompilerParams(
            collective_id=0, has_side_effects=True, vmem_limit_bytes=60 * 1024 * 1024
        ),
    )(
        patches, norm_gain.reshape(1, -1), w_up, bias_up.reshape(1, -1), w_down,
        bias_down.reshape(1, -1), cotangent,
    )
    mlp_out, grad_patches, grad_gain, grad_w_up, grad_bias_up, grad_w_down, grad_bias_down = outs
    return (
        mlp_out, grad_patches, grad_gain.reshape(-1), grad_w_up, grad_bias_up.reshape(-1),
        grad_w_down, grad_bias_down.reshape(-1),
    )


def solution(mesh):
    in_specs = (
        P("gy", "gx"),
        P("gx"),
        P("gx", "gy"),
        P("gy"),
        P("gy", "gx"),
        P("gx"),
        P("gy", "gx"),
    )
    out_specs = (
        P("gy", "gx"),
        P("gy", "gx"),
        P("gx"),
        P("gx", "gy"),
        P("gy"),
        P("gy", "gx"),
        P("gx"),
    )
    return jax.shard_map(shards, mesh=mesh, in_specs=in_specs, out_specs=out_specs, check_vma=False)
```

time: 570 us -> 161 us (0.28)
  waiting for transfers between devices: 429 us -> 0 us
  Pallas kernels: 0 us -> 142 us
  blocking collectives: 71.3 us -> 0 us
  matrix products: 36.4 us -> 0 us
  between operations: 13.8 us -> 0.65 us
  other arithmetic: 16.4 us -> 3.86 us
  local copies, waits for them, and re-layouts: 2.61 us -> 14.1 us
    psum x1 -> x0, waiting for transfers between devices: 262 us -> none  [shards(): hidden = lax.psum(partial_value, 'gx') + bias_up]
    pallas_call x0 -> x1, Pallas kernels: none -> 142 us  [shards(): pl.pallas_call(kernel, out_shape=(shape((64, 768), BF16), shape((64, 768)...]
    all_gather x2 -> x0, waiting for transfers between devices: 91.3 us -> none  [the longest x1 49.5 us: shards(): lax.all_gather(normed, 'gy', axis=0, tiled=True)]
    reduce_scatter x2 -> x0, waiting for transfers between devices: 74.8 us -> none  [the longest x1 53.7 us: shards(): lax.psum_scatter(over_cols(block, w_up), 'gy', scatter_dimension=0, tiled...]
    psum x3 -> x0, blocking collectives: 71.3 us -> none  [the longest x1 39.6 us: shards(): lax.psum((jnp.sum(grad_normed * standard, axis=0), jnp.sum(cotangent, axi...]
    dot_general x6 -> x0, matrix products: 36.4 us -> none  [the longest x2 11.9 us: over_rows(): lax.dot_general(left, right, (((0,), (0,)), ((), ())), preferred_element_...]
    reduce_sum x4 -> x0, other arithmetic: 11.5 us -> none  [the longest x1 9.16 us: shards(): grad_bias_up = jnp.sum(grad_whole, axis=0, dtype=jnp.float32)]
    unnamed x18 -> x8, local copies, waits for them, and re-layouts: 2.61 us -> 10.3 us
  transfers between devices with their start and end apart: 5 -> 0, of which waited for: 5 -> 0; matrix products, arithmetic and copies ran while one was open for 5% -> 0% of each run, Pallas kernels for 0% -> 0%
where the time goes in v1:
time: 161 us; the launch traced here: 160 us
  Pallas kernels  142 us (88%)
  local copies, waits for them, and re-layouts  14.1 us (9%)
  other arithmetic  3.86 us (2%)
    pallas_call x1, Pallas kernels, shards(): pl.pallas_call(kernel, out_shape=(shape((64, 768), BF16), shape((64, 768)...  142 us
    unnamed x8, local copies, waits for them, and re-layouts  10.3 us
    pallas_call x3, other arithmetic, shards(): pl.pallas_call(kernel, out_shape=(shape((64, 768), BF16), shape((64, 768)...  3.86 us

profile of v1, /device:TPU:1, one launch (start us, length us, event | category | flops | bytes accessed | tf_op | source)
XLA Modules:
  0.0 160.5 jit_solution(12332982116954917837)
XLA Ops:
  0.6 1.3 reshape.33.bias_up
  1.9 1.3 reshape.32.gain
  3.2 1.3 reshape.34.bias_down
  4.5 141.8 %shard_map.126 = (bf16[64,768]{1,0:T(8,128)(2,1)}, bf16[64,768]{1,0:T(8,128)(2,1)}, f32[1,768]{1,0:T(1,128)}, f32[768,1536]{1,0:T(8,128)}, f32[1,1536]{1,0:T(1,1...) custom-call(bf16[64,768]{1,0:T(8,128)(2,1)} %patches.1, f32[1,768]{1,0:T(1,128)} %reshape.32.gain, bf16[768,1536]{1,0:T(8,128)(2,1)} %w_up.1, ...), custom_call_target="tpu_custom_call" | custom-call | tf_op jit(solution)/shard_map/pallas_call | solution.py:563
  146.3 1.3 reduce.1
  147.6 1.3 reduce
  148.9 1.3 reduce.2
  150.2 1.5 copy.18
  151.7 0.0 slice-start
  151.7 1.7 %copy.19 = bf16[64,768]{1,0:T(8,128)(2,1)} copy(bf16[64,768]{1,0:T(8,128)(2,1)} %get-tuple-element.29) | data formatting | bytes 196608
  153.4 0.0 slice-start.1
  153.4 4.9 %copy.20 = f32[768,1536]{1,0:T(8,128)} copy(f32[768,1536]{1,0:T(8,128)} %get-tuple-element.31) | data formatting | bytes 9437184
  158.3 0.0 slice-done
  158.3 0.0 slice-done.1
  158.3 2.2 %copy.21 = f32[1536,768]{1,0:T(8,128)} copy(f32[1536,768]{1,0:T(8,128)S(1)} %bitcast.1) | data formatting | bytes 9437184
  (1 shorter events, 0.0 us)
Async XLA Ops:
  151.7 6.6 %slice-start = ((s8[4718592]{0:T(1024)(128)(4,1)}), s8[4194304]{0:T(1024)(128)(4,1)S(1)}, s32[]{:S(2)}) async-start(s8[4718592]{0:T(1024)(128)(4,1)} %bitcast), calls=%async_computation | async-start | bytes 8388608
  153.4 4.9 %slice-start.1 = ((s8[4718592]{0:T(1024)(128)(4,1)}), s8[524288]{0:T(1024)(128)(4,1)S(1)}, s32[]{:S(2)}) async-start(s8[4718592]{0:T(1024)(128)(4,1)} %bitcast), calls=%async_computation.1 | async-start | bytes 1048576

commit v2 on v1

--- a/solution.py
+++ b/solution.py
@@ -22,6 +22,10 @@
 
 def wide(value):
     return value.astype(F32)
+
+
+def row(ref):
+    return ref[...].reshape(1, ref.shape[0])
 
 
 class Mail:
@@ -251,7 +255,7 @@
     def activate(c):
         ga4(c)
         hid4(c)
-        hidden = hid_sum(c, y) + wide(hid_y[c]) + bias_up[...]
+        hidden = hid_sum(c, y) + wide(hid_y[c]) + row(bias_up)
         phi = 0.5 * (1.0 + lax.erf(hidden * inv_root_two))
         act[c, x, y] = (hidden * phi).astype(BF16)
         total = wide(ga[c, x, y]) + wide(ga_y[c, x]) + wide(ga_l[c]) + wide(ga_r[c])
@@ -335,7 +339,7 @@
         back[name, c].wait_recv()
         total = back_sum(name, c, yh) + wide(boxes[name][4][c])
         if name == "mlp":
-            mlp_out[pl.ds(16 * c, 16), :] = (total + bias_down[...]).astype(BF16)
+            mlp_out[pl.ds(16 * c, 16), :] = (total + row(bias_down)).astype(BF16)
         else:
             gn[pl.ds(16 * c, 16), :] = total
 
@@ -345,7 +349,7 @@
     inv_std = lax.rsqrt(square_mean - row_mean * row_mean + epsilon)
     normal = (values - row_mean) * inv_std
     standard[...] = normal
-    normed = (normal * gain[...]).astype(BF16)
+    normed = (normal * row(gain)).astype(BF16)
     for c in range(CHUNKS):
         nor_all[c, yh, z, k] = normed[16 * c : 16 * c + 16]
         to_far("nor", nor_all, c)
@@ -488,7 +492,7 @@
     normal = standard[...]
     weighted = grad_normed * normal
     gains[gy] = jnp.sum(weighted.reshape(8, 8, 768), axis=0)
-    scaled = grad_normed * gain[...]
+    scaled = grad_normed * row(gain)
     stats = post_stats(
         stats_b,
         jnp.sum(scaled, axis=1, keepdims=True),
@@ -505,7 +509,7 @@
         total = total + jnp.sum(wide(gh[c].reshape(256, 1536)), axis=0, keepdims=True)
     grad_bias_up[...] = total
     first_mean, second_mean = read_stats(stats_b, stats)
-    scaled = gn[...] * gain[...]
+    scaled = gn[...] * row(gain)
     grad_patches[...] = (inv_std * (scaled - first_mean - standard[...] * second_mean)).astype(BF16)
     for copy in gain_in:
         copy.wait_recv()
@@ -513,6 +517,39 @@
     mail.finish()
     store_wd.wait()
     store_wu.wait()
+
+
+PIECES = 4
+
+
+def finish(
+    mlp_in, patches_in, gain_in, w_up_in, bias_up_in, w_down_in, bias_down_in,
+    mlp_out, grad_patches, grad_gain, grad_w_up, grad_bias_up, grad_w_down, grad_bias_down,
+    up, down, in_sems, out_sems,
+):
+    moves = []
+    for source, held, target in ((w_down_in, down, grad_w_down), (w_up_in, up, grad_w_up)):
+        height = held.shape[0] // PIECES
+        for p in range(PIECES):
+            piece, at = pl.ds(p * height, height), len(moves)
+            moves.append(
+                (
+                    pltpu.make_async_copy(source.at[piece], held.at[piece], in_sems.at[at]),
+                    pltpu.make_async_copy(held.at[piece], target.at[piece], out_sems.at[at]),
+                )
+            )
+    for load, _ in moves:
+        load.start()
+    mlp_out[...] = mlp_in[...]
+    grad_patches[...] = patches_in[...]
+    grad_gain[...] = gain_in[...].reshape(768)
+    grad_bias_up[...] = bias_up_in[...].reshape(1536)
+    grad_bias_down[...] = bias_down_in[...].reshape(768)
+    for load, store in moves:
+        load.wait()
+        store.start()
+    for _, store in moves:
+        store.wait()
 
 
 def shards(patches, norm_gain, w_up, bias_up, w_down, bias_down, cotangent):
@@ -578,14 +615,29 @@
             collective_id=0, has_side_effects=True, vmem_limit_bytes=60 * 1024 * 1024
         ),
     )(
-        patches, norm_gain.reshape(1, -1), w_up, bias_up.reshape(1, -1), w_down,
-        bias_down.reshape(1, -1), cotangent,
+        patches, norm_gain, w_up, bias_up, w_down, bias_down, cotangent,
     )
-    mlp_out, grad_patches, grad_gain, grad_w_up, grad_bias_up, grad_w_down, grad_bias_down = outs
-    return (
-        mlp_out, grad_patches, grad_gain.reshape(-1), grad_w_up, grad_bias_up.reshape(-1),
-        grad_w_down, grad_bias_down.reshape(-1),
-    )
+    return pl.pallas_call(
+        finish,
+        out_shape=(
+            shape((64, 768), BF16),
+            shape((64, 768), BF16),
+            shape((768,), F32),
+            shape((768, 1536), F32),
+            shape((1536,), F32),
+            shape((1536, 768), F32),
+            shape((768,), F32),
+        ),
+        in_specs=[vmem, vmem, vmem, hbm, vmem, hbm, vmem],
+        out_specs=(vmem, vmem, vmem, hbm, vmem, hbm, vmem),
+        scratch_shapes=[
+            pltpu.VMEM((768, 1536), F32),
+            pltpu.VMEM((1536, 768), F32),
+            pltpu.SemaphoreType.DMA((2 * PIECES,)),
+            pltpu.SemaphoreType.DMA((2 * PIECES,)),
+        ],
+        compiler_params=pltpu.CompilerParams(vmem_limit_bytes=67043328),
+    )(*outs)
 
 
 def solution(mesh):

time: 161 us -> 152 us (0.944)
  local copies, waits for them, and re-layouts: 14.1 us -> 0 us
  Pallas kernels: 142 us -> 151 us
  other arithmetic: 3.86 us -> 0 us
    unnamed x8 -> x0, local copies, waits for them, and re-layouts: 10.3 us -> none
    pallas_call x0 -> x1, Pallas kernels: none -> 8.99 us  [shards(): pl.pallas_call(finish, out_shape=(shape((64, 768), BF16), shape((64, 768)...]
    pallas_call x3 -> x0, other arithmetic: 3.86 us -> none  [shards(): pl.pallas_call(kernel, out_shape=(shape((64, 768), BF16), shape((64, 768)...]
    reshape x3 -> x0, local copies, waits for them, and re-layouts: 3.83 us -> none  [the longest x1 1.3 us: shards(): bias_up.reshape(1, -1)]
where the time goes in v2:
time: 152 us
  Pallas kernels  151 us (99%)
    pallas_call x1, Pallas kernels, shards(): pl.pallas_call(kernel, out_shape=(shape((64, 768), BF16), shape((64, 768)...  142 us
    pallas_call x1, Pallas kernels, shards(): pl.pallas_call(finish, out_shape=(shape((64, 768), BF16), shape((64, 768)...  8.99 us

profile of v2, /device:TPU:1, one launch (start us, length us, event | category | flops | bytes accessed | tf_op | source)
XLA Modules:
  0.0 151.5 jit_solution(11068984816703988635)
XLA Ops:
  0.6 141.9 %shard_map.126 = (bf16[64,768]{1,0:T(8,128)(2,1)}, bf16[64,768]{1,0:T(8,128)(2,1)}, f32[1,768]{1,0:T(1,128)}, f32[768,1536]{1,0:T(8,128)}, f32[1,1536]{1,0:T(1,1...) custom-call(bf16[64,768]{1,0:T(8,128)(2,1)} %patches.1, f32[768]{0:T(1024)} %gain.1, bf16[768,1536]{1,0:T(8,128)(2,1)} %w_up.1, ...), custom_call_target="tpu_custom_call" | custom-call | tf_op jit(solution)/shard_map/pallas_call | solution.py:600
  142.5 9.0 %shard_map.127 = (bf16[64,768]{1,0:T(8,128)(2,1)}, bf16[64,768]{1,0:T(8,128)(2,1)}, f32[768]{0:T(1024)}, f32[768,1536]{1,0:T(8,128)}, f32[1536]{0:T(1024)}, /*index=5*/f32[1536,768]{1,0:T(8,128)}, f32[768]{0:T(1024)}) custom-call(bf16[64,768]{1,0:T(8,128)(2,1)} %get-tuple-element.14.mlp_in, bf16[64,768]{1,0:T(8,128)(2,1)} %get-tuple-element.15.patches_in, ...), custom_call_target="tpu_custom_call" | custom-call | tf_op jit(solution)/shard_map/pallas_call | solution.py:620

commit v3 on v2

--- a/solution.py
+++ b/solution.py
@@ -9,6 +9,8 @@
 
 D = 6144
 CHUNKS = 4
+GA_X = (0,)
+GH_Y = (3,)
 MESSAGES = 240
 
 epsilon = 1e-06
@@ -56,6 +58,7 @@
     mlp_out, grad_patches, grad_gain, grad_w_up, grad_bias_up, grad_w_down, grad_bias_down,
     own, standard, wu, wd, cot_all, nor_all,
     ga, ga_y, ga_m1r, ga_m1l, ga_l, ga_r,
+    gax_m1r, gax_m1l, gax_l, gax_r, gax_ys, gax_y,
     hid, hid_m1r, hid_m1l, hid_l, hid_r, hid_ys, hid_y,
     act, gh,
     mlp_g, mlp_sib, mlp_z, mlp_ys, mlp_y,
@@ -223,65 +226,85 @@
         for copy in ga_in[c]:
             copy.wait_recv()
 
-    def hid1(c):
-        hid_in[c] = [
-            mail.send(hid.at[c, xo, 0], hid_m1r.at[c], right),
-            mail.send(hid.at[c, xo, 1], hid_m1l.at[c], left),
-            mail.send(hid.at[c, xr, 1], hid_l.at[c, 1], right),
-            mail.send(hid.at[c, xl, 0], hid_r.at[c, 0], left),
-        ]
-
-    def hid2(c):
-        hid_in[c][0].wait_recv()
-        hid[c, xr, 0] = (wide(hid[c, xr, 0]) + wide(hid_m1r[c])).astype(BF16)
-        first = mail.send(hid.at[c, xr, 0], hid_l.at[c, 0], right)
-        hid_in[c][1].wait_recv()
-        hid[c, xl, 1] = (wide(hid[c, xl, 1]) + wide(hid_m1l[c])).astype(BF16)
-        second = mail.send(hid.at[c, xl, 1], hid_r.at[c, 1], left)
-        hid_in[c] = hid_in[c][2:] + [first, second]
-
-    def hid_sum(c, at):
-        return wide(hid[c, x, at]) + wide(hid_l[c, at]) + wide(hid_r[c, at])
-
-    def hid3(c):
-        for copy in hid_in[c]:
-            copy.wait_recv()
-        hid_ys[c] = hid_sum(c, yo).astype(BF16)
-        hid_in[c] = [mail.send(hid_ys.at[c], hid_y.at[c], across)]
-
-    def hid4(c):
-        hid_in[c][0].wait_recv()
+    def x_sum(part, l, r, c, at):
+        return wide(part[c, x, at]) + wide(l[c, at]) + wide(r[c, at])
+
+    def x_first(part, m1r, m1l, l, r, ys, y_box, came):
+        def one(c):
+            came[c] = [
+                mail.send(part.at[c, xo, 0], m1r.at[c], right),
+                mail.send(part.at[c, xo, 1], m1l.at[c], left),
+                mail.send(part.at[c, xr, 1], l.at[c, 1], right),
+                mail.send(part.at[c, xl, 0], r.at[c, 0], left),
+            ]
+
+        def two(c):
+            came[c][0].wait_recv()
+            part[c, xr, 0] = (wide(part[c, xr, 0]) + wide(m1r[c])).astype(BF16)
+            first = mail.send(part.at[c, xr, 0], l.at[c, 0], right)
+            came[c][1].wait_recv()
+            part[c, xl, 1] = (wide(part[c, xl, 1]) + wide(m1l[c])).astype(BF16)
+            second = mail.send(part.at[c, xl, 1], r.at[c, 1], left)
+            came[c] = came[c][2:] + [first, second]
+
+        def three(c):
+            for copy in came[c]:
+                copy.wait_recv()
+            ys[c] = x_sum(part, l, r, c, yo).astype(BF16)
+            came[c] = [mail.send(ys.at[c], y_box.at[c], across)]
+
+        def four(c):
+            came[c][0].wait_recv()
+
+        return one, two, three, four
+
+    hid1, hid2, hid3, hid4 = x_first(
+        hid, hid_m1r, hid_m1l, hid_l, hid_r, hid_ys, hid_y, hid_in
+    )
+    gax = x_first(ga, gax_m1r, gax_m1l, gax_l, gax_r, gax_ys, gax_y, ga_in)
+    gay = (ga1, ga2, ga3, ga4)
+
+    def ga_step(n, c):
+        (gax if c in GA_X else gay)[n - 1](c)
 
     def activate(c):
-        ga4(c)
+        ga_step(4, c)
         hid4(c)
-        hidden = hid_sum(c, y) + wide(hid_y[c]) + row(bias_up)
+        hidden = x_sum(hid, hid_l, hid_r, c, y) + wide(hid_y[c]) + row(bias_up)
         phi = 0.5 * (1.0 + lax.erf(hidden * inv_root_two))
         act[c, x, y] = (hidden * phi).astype(BF16)
-        total = wide(ga[c, x, y]) + wide(ga_y[c, x]) + wide(ga_l[c]) + wide(ga_r[c])
+        if c in GA_X:
+            total = x_sum(ga, gax_l, gax_r, c, y) + wide(gax_y[c])
+        else:
+            total = wide(ga[c, x, y]) + wide(ga_y[c, x]) + wide(ga_l[c]) + wide(ga_r[c])
         slope = phi + hidden * jnp.exp(-0.5 * hidden * hidden) * inv_root_two_pi
         gh[c, x, y] = (total * slope).astype(BF16)
 
-    def act1(c):
-        piece = act.at[c, x, y]
-        act_in[c] = [mail.send(piece, piece, device) for device in (across, right, left)]
-
-    def act2(c):
-        act_in[c][0].wait_recv()
-        piece = act.at[c, x, yo]
-        act_in[c] = act_in[c][1:] + [mail.send(piece, piece, device) for device in (right, left)]
-
-    def act3(c):
-        for copy in act_in[c]:
-            copy.wait_recv()
-        act_in[c] = [
-            mail.send(act.at[c, xl, 0], act.at[c, xl, 0], right),
-            mail.send(act.at[c, xr, 1], act.at[c, xr, 1], left),
-        ]
-
-    def act4(c):
-        for copy in act_in[c]:
-            copy.wait_recv()
+    def y_gather(full, came):
+        def one(c):
+            piece = full.at[c, x, y]
+            came[c] = [mail.send(piece, piece, device) for device in (across, right, left)]
+
+        def two(c):
+            came[c][0].wait_recv()
+            piece = full.at[c, x, yo]
+            came[c] = came[c][1:] + [mail.send(piece, piece, device) for device in (right, left)]
+
+        def three(c):
+            for copy in came[c]:
+                copy.wait_recv()
+            came[c] = [
+                mail.send(full.at[c, xl, 0], full.at[c, xl, 0], right),
+                mail.send(full.at[c, xr, 1], full.at[c, xr, 1], left),
+            ]
+
+        def four(c):
+            for copy in came[c]:
+                copy.wait_recv()
+
+        return one, two, three, four
+
+    act1, act2, act3, act4 = y_gather(act, act_in)
 
     def gh1(c):
         piece = gh.at[c, x, y]
@@ -305,6 +328,11 @@
     def gh4(c):
         for copy in gh_in[c]:
             copy.wait_recv()
+
+    ghy, ghx = y_gather(gh, gh_in), (gh1, gh2, gh3, gh4)
+
+    def gh_step(n, c):
+        (ghy if c in GH_Y else ghx)[n - 1](c)
 
     boxes = {"mlp": (mlp_g, mlp_sib, mlp_z, mlp_ys, mlp_y), "gn": (gn_g, gn_sib, gn_z, gn_ys, gn_y)}
     back = {}
@@ -362,7 +390,7 @@
 
     def start_ga(c):
         make_ga(c)
-        ga1(c)
+        ga_step(1, c)
 
     def start_hid(c):
         make_hid(c)
@@ -371,7 +399,7 @@
     def start_act(c):
         activate(c)
         act1(c)
-        gh1(c)
+        gh_step(1, c)
 
     def start_mlp(c):
         act4(c)
@@ -379,7 +407,7 @@
         back0("mlp", c)
 
     def start_gn(c):
-        gh4(c)
+        gh_step(4, c)
         make_gn(c)
         back0("gn", c)
 
@@ -397,40 +425,40 @@
     start_ga(1)
     cot3(2)
     nor3(0)
-    ga2(0)
+    ga_step(2, 0)
     start_hid(0)
     start_ga(2)
     cot3(3)
     nor3(1)
-    ga3(0)
-    ga2(1)
+    ga_step(3, 0)
+    ga_step(2, 1)
     hid2(0)
     start_hid(1)
     start_ga(3)
     nor3(2)
-    ga3(1)
-    ga2(2)
+    ga_step(3, 1)
+    ga_step(2, 2)
     hid3(0)
     hid2(1)
     start_hid(2)
     start_act(0)
     nor3(3)
-    ga3(2)
-    ga2(3)
+    ga_step(3, 2)
+    ga_step(2, 3)
     hid3(1)
     hid2(2)
     act2(0)
     start_hid(3)
     start_act(1)
-    gh2(0)
-    ga3(3)
+    gh_step(2, 0)
+    ga_step(3, 3)
     hid3(2)
     hid2(3)
     act3(0)
     act2(1)
     start_act(2)
-    gh3(0)
-    gh2(1)
+    gh_step(3, 0)
+    gh_step(2, 1)
     hid3(3)
     start_mlp(0)
     act3(1)
@@ -438,8 +466,8 @@
     start_act(3)
     start_gn(0)
     grad_down(0)
-    gh3(1)
-    gh2(2)
+    gh_step(3, 1)
+    gh_step(2, 2)
     back1("mlp", 0)
     start_mlp(1)
     act3(2)
@@ -447,8 +475,8 @@
     back1("gn", 0)
     grad_up(0)
     start_gn(1)
-    gh3(2)
-    gh2(3)
+    gh_step(3, 2)
+    gh_step(2, 3)
     back2("mlp", 0)
     back1("mlp", 1)
     grad_down(1)
@@ -457,7 +485,7 @@
     back2("gn", 0)
     back1("gn", 1)
     start_gn(2)
-    gh3(3)
+    gh_step(3, 3)
     grad_up(1)
     back3("mlp", 0)
     back2("mlp", 1)
@@ -566,6 +594,12 @@
         pltpu.VMEM((4, 4, 32, 1536), BF16),
         pltpu.VMEM((4, 16, 1536), BF16),
         pltpu.VMEM((4, 16, 1536), BF16),
+        pltpu.VMEM((4, 32, 1536), BF16),
+        pltpu.VMEM((4, 32, 1536), BF16),
+        pltpu.VMEM((4, 32, 1536), BF16),
+        pltpu.VMEM((4, 32, 1536), BF16),
+        pltpu.VMEM((4, 2, 32, 1536), BF16),
+        pltpu.VMEM((4, 2, 32, 1536), BF16),
         pltpu.VMEM((4, 32, 1536), BF16),
         pltpu.VMEM((4, 32, 1536), BF16),
         pltpu.VMEM((4, 4, 2, 32, 1536), BF16),

time: 152 us -> 147 us (0.967)
  Pallas kernels: 151 us -> 146 us
    pallas_call x1, Pallas kernels: 142 us -> 137 us  [shards(): pl.pallas_call(kernel, out_shape=(shape((64, 768), BF16), shape((64, 768)...]
where the time goes in v3:
time: 147 us
  Pallas kernels  146 us (99%)
    pallas_call x1, Pallas kernels, shards(): pl.pallas_call(kernel, out_shape=(shape((64, 768), BF16), shape((64, 768)...  137 us
    pallas_call x1, Pallas kernels, shards(): pl.pallas_call(finish, out_shape=(shape((64, 768), BF16), shape((64, 768)...  8.99 us

profile of v3, /device:TPU:1, one launch (start us, length us, event | category | flops | bytes accessed | tf_op | source)
XLA Modules:
  0.0 147.0 jit_solution(1592631989956716982)
XLA Ops:
  0.6 137.4 %shard_map.126 = (bf16[64,768]{1,0:T(8,128)(2,1)}, bf16[64,768]{1,0:T(8,128)(2,1)}, f32[1,768]{1,0:T(1,128)}, f32[768,1536]{1,0:T(8,128)}, f32[1,1536]{1,0:T(1,1...) custom-call(bf16[64,768]{1,0:T(8,128)(2,1)} %patches.1, f32[768]{0:T(1024)} %gain.1, bf16[768,1536]{1,0:T(8,128)(2,1)} %w_up.1, ...), custom_call_target="tpu_custom_call" | custom-call | tf_op jit(solution)/shard_map/pallas_call | solution.py:634
  138.0 9.0 %shard_map.127 = (bf16[64,768]{1,0:T(8,128)(2,1)}, bf16[64,768]{1,0:T(8,128)(2,1)}, f32[768]{0:T(1024)}, f32[768,1536]{1,0:T(8,128)}, f32[1536]{0:T(1024)}, /*index=5*/f32[1536,768]{1,0:T(8,128)}, f32[768]{0:T(1024)}) custom-call(bf16[64,768]{1,0:T(8,128)(2,1)} %get-tuple-element.14.mlp_in, bf16[64,768]{1,0:T(8,128)(2,1)} %get-tuple-element.15.patches_in, ...), custom_call_target="tpu_custom_call" | custom-call | tf_op jit(solution)/shard_map/pallas_call | solution.py:654
